TPU v7x, 128 devices: a whole 4x4x4 slice. The times are simulated.
128 devices in a mesh: tm: 32 (over x, z, core), space: 4 (over y).
Axes of the slice: x: 4, y: 4, z: 4, core: 2. Of those that a mesh axis runs over, the one named last changes fastest.
Arguments:
- observations: bfloat16 [8192, 32, 4, 512], P(None, 'tm', 'space'), may hold values from -6 to 6
- pod_basis: bfloat16 [32, 4, 512, 1024], P(None, 'space'), may hold values from -0.0234375 to 0.0234375
- decay: float32 [8192, 1024], P('tm', 'space'), may hold values from 0 to 1
- step_mask: int32 [8192], P('tm'), may hold values 0 or 1
- process_var: float32 [1024], P('space'), may hold values from 0.00012207031 to 1
- obs_var: float32 [1024], P('space'), may hold values from 1 to 512
- prior_mean: float32 [1024], P('space'), may hold values from -6 to 6
- prior_var: float32 [1024], P('space'), may hold values from 0.5 to 4
Outputs:
- coefficients: float32 [8192, 1024], P('tm', 'space')
- filtered_mean: float32 [8192, 1024], P('tm', 'space')
- smoothed_mean: float32 [8192, 1024], P('tm', 'space')
- log_variance: float32 [8192, 1024], P('tm', 'space')
All inputs are finite; a program needn't handle non-finite values. No bound on the sum of `step_mask` on one device may be relied on, other than what follows from the above.
Results may differ from a plain program's by a relative error of at most 0.0003.
Values may be sent and summed in bfloat16 or wider, within the bound.
A program may use at most 256 MiB of HBM per device.

v0:
```python
import jax
import jax.numpy as jnp
from jax import lax
from jax.sharding import PartitionSpec as P


def entering(value, axis, join, neutral, backward):
    count, mine = (lax.axis_size(axis), lax.axis_index(axis))
    pieces = jax.tree.map(lambda part: lax.all_gather(part, axis), value)
    if backward:
        pieces = jax.tree.map(lambda part: part[::-1], pieces)
        mine = count - 1 - mine
    running = jax.tree.map(
        lambda part, zero: jnp.full_like(part, 0) + jnp.asarray(zero, part.dtype), value, neutral
    )

    def turn(position, running):
        longer = join(running, jax.tree.map(lambda part: part[position], pieces))
        return jax.tree.map(lambda new, old: jnp.where(position < mine, new, old), longer, running)

    return lax.fori_loop(0, count - 1, turn, running)


def shifted(block, axis, distance):
    devices = range(lax.axis_size(axis))
    route = [(i - distance, i) for i in devices if i - distance in devices]
    return lax.ppermute(block, axis, route)


def filter_combine(early, late):
    lead_early, base_early, spread_early, pull_early, weight_early = early
    lead_late, base_late, spread_late, pull_late, weight_late = late
    factor = 1.0 / (1.0 + spread_early * weight_late)
    return (
        lead_late * factor * lead_early,
        lead_late * factor * (base_early + spread_early * pull_late) + base_late,
        lead_late * lead_late * factor * spread_early + spread_late,
        lead_early * factor * (pull_late - weight_late * base_early) + pull_early,
        lead_early * lead_early * factor * weight_late + weight_early,
    )


def smooth_combine(early, late):
    gain_early, offset_early, spread_early = early
    gain_late, offset_late, spread_late = late
    return (
        gain_early * gain_late,
        gain_early * offset_late + offset_early,
        gain_early * gain_early * spread_late + spread_early,
    )


def smooth_backward(later, earlier):
    return smooth_combine(earlier, later)


def suffix_scan(elements):
    flipped = tuple((part_rows[::-1] for part_rows in elements))
    scanned = lax.associative_scan(smooth_backward, flipped, axis=0)
    return tuple((part_rows[::-1] for part_rows in scanned))


def body(observations, pod_basis, decay, step_mask, process_var, obs_var, prior_mean, prior_var):
    tm_count = lax.axis_size("tm")
    space_count = lax.axis_size("space")
    steps_local = decay.shape[0]
    modes_local = decay.shape[1]
    position = lax.axis_index("tm")
    own_slab = observations.reshape(tm_count, steps_local, observations.shape[3])
    own_basis = lax.dynamic_index_in_dim(pod_basis, position, 0, keepdims=False)
    own_basis = own_basis.reshape(-1, space_count, modes_local)
    terms = jnp.einsum("tsc,cnk->tnsk", own_slab, own_basis, preferred_element_type=jnp.float32)
    terms = terms.reshape(tm_count * space_count, steps_local, modes_local)
    coefficients = lax.psum_scatter(terms, ("tm", "space"), scatter_dimension=0, tiled=True)[0]
    observed = step_mask.astype(jnp.float32)[:, None]
    row_index = lax.broadcasted_iota(jnp.int32, (steps_local, 1), 0)
    opening = (row_index == 0) & (position == 0)
    transit = jnp.where(opening, 0.0, decay)
    base_mean = jnp.where(opening, prior_mean[None, :], 0.0)
    base_var = jnp.where(opening, prior_var[None, :], process_var[None, :])
    denominator = base_var + obs_var[None, :]
    kalman_gain = observed * base_var / denominator
    retain = (obs_var[None, :] + (1.0 - observed) * base_var) / denominator
    elements = (
        retain * transit,
        base_mean + kalman_gain * (coefficients - base_mean),
        retain * base_var,
        observed * transit * coefficients / denominator,
        observed * transit * transit / denominator,
    )
    local_prefix = lax.associative_scan(filter_combine, elements, axis=0)
    totals = tuple((part_rows[-1:] for part_rows in local_prefix))
    unit = jnp.ones_like(totals[0])
    blank = jnp.zeros_like(totals[0])
    filter_unit = (unit, blank, blank, blank, blank)
    before = entering(totals, "tm", filter_combine, filter_unit, False)
    filtered = filter_combine(before, local_prefix)
    filtered_mean = filtered[1]
    filtered_var = filtered[2]
    following = shifted(decay[:1], "tm", -1)
    next_decay = jnp.concatenate([decay[1:], following], 0)
    predicted = next_decay * next_decay * filtered_var + process_var[None, :]
    smoother_gain = filtered_var * next_decay / predicted
    pieces = (
        smoother_gain,
        filtered_mean - smoother_gain * next_decay * filtered_mean,
        filtered_var * process_var[None, :] / predicted,
    )
    local_suffix = suffix_scan(pieces)
    heads = tuple((part_rows[:1] for part_rows in local_suffix))
    smooth_unit = (unit, blank, blank)
    after = entering(heads, "tm", smooth_backward, smooth_unit, True)
    smoothed = smooth_combine(local_suffix, after)
    return (coefficients, filtered_mean, smoothed[1], jnp.log(smoothed[2]))


def solution(mesh):
    return jax.shard_map(
        body,
        mesh=mesh,
        in_specs=(
            P(None, "tm", "space", None),
            P(None, "space", None, None),
            P("tm", "space"),
            P("tm"),
            P("space"),
            P("space"),
            P("space"),
            P("space"),
        ),
        out_specs=(P("tm", "space"), P("tm", "space"), P("tm", "space"), P("tm", "space")),
        check_vma=False,
    )
```

profile of v0, /device:TPU:1, one launch (start us, length us, event | category | flops | bytes accessed | tf_op | source)
XLA Modules:
  0.0 1007.6 jit_solution(16554531158576561588)
XLA Ops:
  7.2 1.3 constant_dynamic-slice_fusion.6
  9.1 18.7 %convolution_bitcast_fusion = f32[32,4,256,256]{2,3,0,1:T(8,128)} fusion(bf16[512,4,256,1]{0,2,3,1:T(8,128)(2,1)S(1)} %bitcast.121, bf16[32,256,512,1]{2,1,0,3:T(8,128)(2,1)} %bitcast.134), kind=kOutput, calls=%fused_computation.32 | convolution fusion | flops 8589934592 | bytes 42991616 | tf_op jit(solution)/shard_map/tsc,cnk->tnsk/dot_general | solution.py:72
  27.8 33.4 %copy.16 = f32[32,4,256,256]{3,2,1,0:T(8,128)} copy(f32[32,4,256,256]{2,3,0,1:T(8,128)} %convolution_bitcast_fusion) | data formatting | bytes 67108864 | tf_op jit(solution)/shard_map/tsc,cnk->tnsk/transpose | solution.py:72
  61.2 0.9 copy-done
  62.7 3.3 collective-permute-start
  66.1 691.6 %reduce-scatter.2.cloned.1.call-done = f32[1,256,256]{2,1,0:T(8,128)} async-done(((f32[128,256,256]{2,1,0:T(8,128)}), f32[1,256,256]{2,1,0:T(8,128)}) %reduce-scatter.2.cloned.1.call-update) | async-done | bytes 262160 | tf_op jit(solution)/shard_map/reduce_scatter | solution.py:74
  757.7 1.2 select_add_fusion.1
  759.9 0.7 slice.994
  760.6 1.0 multiply_add_fusion.9
  769.8 31.0 %all-gather.12 = f32[32,1,256]{2,1,0:T(1,128)} all-gather(f32[1,1,256]{2,1,0:T(1,128)S(1)} %add_bitcast_fusion.3), channel_id=6, replica_groups=mesh['tm'=32,'space'=4] {'tm'}, dimensions={0}, use_global_device_ids=true | all-gather | bytes 33792 | tf_op jit(solution)/shard_map/all_gather | solution.py:9
  802.8 1.0 pad.469
  803.8 25.1 %all-gather.11 = f32[32,1,256]{2,1,0:T(1,128)S(1)} all-gather(f32[1,1,256]{2,1,0:T(1,128)S(1)} %add_bitcast_fusion.4), channel_id=5, replica_groups=mesh['tm'=32,'space'=4] {'tm'}, dimensions={0}, use_global_device_ids=true | all-gather | bytes 33792 | tf_op jit(solution)/shard_map/all_gather | solution.py:9
  829.7 21.8 %all-gather.10 = f32[32,1,256]{2,1,0:T(1,128)S(1)} all-gather(f32[1,1,256]{2,1,0:T(1,128)S(1)} %add_bitcast_fusion.5), channel_id=4, replica_groups=mesh['tm'=32,'space'=4] {'tm'}, dimensions={0}, use_global_device_ids=true | all-gather | bytes 33792 | tf_op jit(solution)/shard_map/all_gather | solution.py:9
  852.2 23.9 %all-gather.9 = f32[32,1,256]{2,1,0:T(1,128)S(1)} all-gather(f32[1,1,256]{2,1,0:T(1,128)S(1)} %add_bitcast_fusion.6), channel_id=3, replica_groups=mesh['tm'=32,'space'=4] {'tm'}, dimensions={0}, use_global_device_ids=true | all-gather | bytes 33792 | tf_op jit(solution)/shard_map/all_gather | solution.py:9
  876.9 21.9 %all-gather.8 = f32[32,1,256]{2,1,0:T(1,128)S(1)} all-gather(f32[1,1,256]{2,1,0:T(1,128)S(1)} %add_bitcast_fusion.7), channel_id=2, replica_groups=mesh['tm'=32,'space'=4] {'tm'}, dimensions={0}, use_global_device_ids=true | all-gather | bytes 33792 | tf_op jit(solution)/shard_map/all_gather | solution.py:9
  898.8 21.7 %while.32 = (s32[]{:T(128)}, f32[1,256]{1,0:T(1,128)S(1)}, f32[1,256]{1,0:T(1,128)S(1)}, s32[]{:T(128)}, f32[32,1,256]{2,1,0:T(1,128)S(1)}, /*index=5*/f32[32,1,...) while((s32[]{:T(128)}, f32[1,256]{1,0:T(1,128)S(1)}, ...), condition=%wide.region_2.3_spmd.clone, body=%wide.region_1.2_spmd.clone.sunk | while | flops 4100 | bytes 9349 | solution.py:21
  900.2 0.7 broadcast_select_fusion.10
  903.6 0.7 broadcast_select_fusion.10
  905.1 0.7 broadcast_select_fusion.10
  907.2 0.7 broadcast_select_fusion.10
  907.9 0.7 broadcast_select_fusion.10
  911.4 0.7 broadcast_select_fusion.10
  914.9 0.7 broadcast_select_fusion.10
  916.3 0.7 broadcast_select_fusion.10
  917.0 0.7 broadcast_select_fusion.10
  920.6 0.8 multiply_divide_fusion
  921.4 1.6 multiply_subtract_fusion
  928.5 23.9 %all-gather.15 = f32[32,1,256]{2,1,0:T(1,128)S(1)} all-gather(f32[1,1,256]{2,1,0:T(1,128)S(1)} %add_bitcast_fusion), channel_id=9, replica_groups=mesh['tm'=32,'space'=4] {'tm'}, dimensions={0}, use_global_device_ids=true | all-gather | bytes 33792 | tf_op jit(solution)/shard_map/all_gather | solution.py:9
  952.4 21.7 %all-gather.14 = f32[32,1,256]{2,1,0:T(1,128)S(1)} all-gather(f32[1,1,256]{2,1,0:T(1,128)S(1)} %add_bitcast_fusion.1), channel_id=8, replica_groups=mesh['tm'=32,'space'=4] {'tm'}, dimensions={0}, use_global_device_ids=true | all-gather | bytes 33792 | tf_op jit(solution)/shard_map/all_gather | solution.py:9
  974.2 23.9 %all-gather.13 = f32[32,1,256]{2,1,0:T(1,128)S(1)} all-gather(f32[1,1,256]{2,1,0:T(1,128)S(1)} %add_bitcast_fusion.2), channel_id=7, replica_groups=mesh['tm'=32,'space'=4] {'tm'}, dimensions={0}, use_global_device_ids=true | all-gather | bytes 33792 | tf_op jit(solution)/shard_map/all_gather | solution.py:9
  998.2 1.5 while.33
  999.9 0.9 add_log_fusion
  (577 shorter events, 33.6 us)
Async XLA Ops:
  7.2 750.5 %reduce-scatter.2.cloned.1.call-start = ((), (), s32[]{:S(2)}) async-start(), calls=%async_computation.1 | async-start | bytes 33816576 | tf_op jit(solution)/shard_map/reduce_scatter | solution.py:74
  61.2 0.9 copy-start
  61.2 4.9 copy-start.2
  61.2 696.5 %copy-start.1 = (f32[256]{0:T(256)S(1)}, f32[256]{0:T(256)}, u32[]{:S(2)}) copy-start(f32[256]{0:T(256)} %param.16) | copy-start | bytes 3076
  61.2 696.5 %copy-start.3 = (f32[256]{0:T(256)S(1)}, f32[256]{0:T(256)}, u32[]{:S(2)}) copy-start(f32[256]{0:T(256)} %param.18) | copy-start | bytes 3076
  61.2 696.5 %copy-start.4 = (f32[256]{0:T(256)S(1)}, f32[256]{0:T(256)}, u32[]{:S(2)}) copy-start(f32[256]{0:T(256)} %param.19) | copy-start | bytes 3076
  61.2 696.5 %copy-start.5 = (f32[256]{0:T(256)S(1)}, f32[256]{0:T(256)}, u32[]{:S(2)}) copy-start(f32[256]{0:T(256)} %param.17) | copy-start | bytes 3076
  62.7 857.8 %collective-permute-start = (f32[1,256]{1,0:T(1,128)}, f32[1,256]{1,0:T(1,128)}, u32[]{:S(2)}, u32[]{:S(2)}) collective-permute-start(f32[1,256]{1,0:T(1,128)} %slice.1174), channel_id=1, source_target_pairs={{4,0},{8,4},{12,8},{16,12},{20,16},{24,20},{28,24},{32,28},{36,32}... | collective-permute-start | bytes 3080 | tf_op jit(solution)/shard_map/ppermute | solution.py:27
Sparse Core Ops, SparseCore 0:
  61.4 696.2 reduce-scatter.1
where the time goes:
time: 1010 us
  waiting for transfers between devices  692 us (69%)
  blocking collectives  193 us (19%)
  local copies, waits for them, and re-layouts  49.7 us (5%)
  other arithmetic  32.9 us (3%)
  matrix products  18.7 us (2%)
  between operations  16.8 us (2%)
    reduce_scatter x1, waiting for transfers between devices, body(): lax.psum_scatter(terms, ('tm', 'space'), scatter_dimension=0, tiled=True)[0]  692 us
    all_gather x8, blocking collectives, entering(): pieces = jax.tree.map(lambda part: lax.all_gather(part, axis), value)  193 us
    transpose x1, local copies, waits for them, and re-layouts, body(): jnp.einsum('tsc,cnk->tnsk', own_slab, own_basis, preferred_element_type=j...  33.4 us
    select_n x62, other arithmetic, turn(): jnp.where(position < mine, new, old)  21.8 us
  transfers between devices with their start and end apart: 2, of which 1 were waited for; matrix products, arithmetic and copies ran while one was open for 4% of the time, Pallas kernels for 0%

commit v1 on v0

v1 whole, which is shorter than its diff:
```python
import jax
import jax.numpy as jnp
from jax import lax
from jax.experimental import pallas as pl
from jax.experimental.pallas import tpu as pltpu
from jax.sharding import PartitionSpec as P

MESH = pl.DeviceIdType.MESH
F32 = jnp.float32
BF16 = jnp.bfloat16
I16 = jnp.int16

UNIT = (96, 80, 80)
START = (0, 96, 176)
ORDER = (("x", "y", "z"), ("y", "z", "x"), ("z", "x", "y"))
ROWS = tuple(64 * u for u in UNIT)
LIMIT = 32760.0
TINY = 1e-33

MESSAGES = ((2, 0, 1), (2, 1, -1), (1, 0, 1), (1, 1, 1), (3, 0, -1), (3, 1, -1))


def stage_rows(part, stage):
    return ROWS[part] // 4 ** (stage + 1)


def half_rows(part, stage, half):
    rows = stage_rows(part, stage)
    first = rows // 2 if stage < 2 else 48
    return (0, first) if half == 0 else (first, rows - first)


def chunk_rows(part, rows):
    return UNIT[part] if rows % UNIT[part] == 0 else rows


def kernel(obs, basis, decay, mask, q_ref, r_ref, pm_ref, pv_ref, coef_out, fm_out, sm_out, lv_out, *scratch):
    (fa, fb, fc, qa, qb, qc, ra1, ra2, ra3, rb1, rb2, rb3, rc1, rc2, rc3, oa, ob, oc, bas, scale_out, scale_in,
     dec, flag, qv, vv, aa, kk, gg, ww, ap, sm, gs, sv, cc, ll, s0, small, e1, e2, e3, g1, g2, g3, mi,
     own_sem, part_sem, psend_sem, bas_sem, send_sem, recv_sem, ssend_sem, srecv_sem, esend_sem, erecv_sem) = scratch
    acc = (fa, fb, fc)
    quant = (qa, qb, qc)
    landed = ((ra1, ra2, ra3), (rb1, rb2, rb3), (rc1, rc2, rc3))
    tm = lax.axis_index("tm")
    y = lax.axis_index("space")
    x, z, core = tm // 8, lax.rem(tm // 2, 4), lax.rem(tm, 2)
    partner = tm + 1 - 2 * core

    def turn(value, by, count):
        return lax.rem(value + by, count)

    def neighbour(axis, way):
        if axis == "x":
            return {"tm": turn(tm, 8 if way > 0 else 24, 32)}
        if axis == "z":
            return {"tm": x * 8 + turn(z, 1 if way > 0 else 3, 4) * 2 + core}
        return {"space": turn(y, 1 if way > 0 else 3, 4)}

    barrier = pltpu.get_barrier_semaphore()

    def greet(step, carry):
        pl.semaphore_signal(barrier, inc=1, device_id={"tm": turn(tm, step, 32)}, device_id_type=MESH)
        return carry

    lax.fori_loop(1, 32, greet, 0)
    for way in (1, -1):
        pl.semaphore_signal(barrier, inc=1, device_id=neighbour("y", way), device_id_type=MESH)

    def obs_copies(part, slot):
        rows = slice(START[part], START[part] + UNIT[part])
        pieces = []
        for other in range(4):
            if part == 0:
                at, to = (turn(x, slot, 4), turn(z, other, 4)), oa.at[slot, other]
            elif part == 1:
                at, to = (turn(x, other, 4), turn(z, slot, 4)), ob.at[slot, other]
            else:
                at, to = (turn(x, other, 4), turn(z, slot, 4)), oc.at[slot, other]
            pieces.append((at, rows, to))
        return pieces

    tasks = [(0, 2), (1, 0), (1, 1), (1, 2), (1, 3), (2, 2), (0, 1), (0, 3), (2, 1), (2, 3), (0, 0), (2, 0)]
    held = (oa, ob, oc)
    for yr in range(4):
        columns = pl.ds(pl.multiple_of(turn(y, yr, 4) * 256, 256), 256)
        for side, who in ((0, tm), (1, partner)):
            pltpu.make_async_copy(
                basis.at[who, :, columns], bas.at[yr, pl.ds(side * 512, 512)], bas_sem.at[yr]
            ).start()
    for part, slot in tasks:
        for (xi, zi), rows, to in obs_copies(part, slot):
            pltpu.make_async_copy(obs.at[xi, zi, core, rows], to.at[:, 0:512], own_sem.at[part, slot]).start()

    dec[0, 0:256, :] = decay[:, 0:128]
    dec[1, 0:256, :] = decay[:, 128:256]
    first = tm == 0
    for h in range(2):
        lanes = slice(h * 128, h * 128 + 128)
        e1[3:4, lanes] = dec[h, 0:1, :]
        qv[h] = jnp.broadcast_to(q_ref[:, lanes], (256, 128))
        qv[h, 0:1, :] = jnp.where(first, pv_ref[:, lanes], q_ref[:, lanes])
        dec[h, 0:1, :] = jnp.where(first, 0.0, dec[h, 0:1, :])
    row = lax.broadcasted_iota(jnp.int32, (256, 256), 0)
    column = lax.broadcasted_iota(jnp.int32, (256, 256), 1)
    spread_mask = jnp.where(row == column, jnp.broadcast_to(mask[...].astype(F32), (256, 256)), 0.0).astype(BF16)
    flag[...] = jnp.dot(spread_mask, jnp.ones((256, 128), BF16), preferred_element_type=F32)

    noise = [jnp.broadcast_to(r_ref[:, h * 128 : h * 128 + 128], (8, 128)) for h in range(2)]
    process = [jnp.broadcast_to(q_ref[:, h * 128 : h * 128 + 128], (8, 128)) for h in range(2)]

    def steps(s):
        return pl.ds(s, 8, stride=32)

    def join(early, late):
        lead_e, spread_e, weight_e = early
        lead_l, spread_l, weight_l = late
        factor = 1.0 / (1.0 + spread_e * weight_l)
        return (
            lead_l * factor * lead_e,
            lead_l * lead_l * factor * spread_e + spread_l,
            lead_e * lead_e * factor * weight_l + weight_e,
        )

    def compose(s, carry):
        seen = flag[steps(s), :]
        out = []
        for h in range(2):
            d, q = dec[h, steps(s), :], qv[h, steps(s), :]
            den = 1.0 / (q + noise[h])
            retain = (noise[h] + (1.0 - seen) * q) * den
            out.append(join(carry[h], (retain * d, retain * q, seen * d * d * den)))
        return tuple(out)

    one, nil = jnp.ones((8, 128), F32), jnp.zeros((8, 128), F32)
    chunks = lax.fori_loop(0, 32, compose, ((one, nil, nil), (one, nil, nil)))
    for h in range(2):
        lanes = slice(h * 128, h * 128 + 128)
        total = tuple(part[0:1] for part in chunks[h])
        for k in range(1, 8):
            total = join(total, tuple(part[k : k + 1] for part in chunks[h]))
        for i in range(3):
            e1[i : i + 1, lanes] = total[i]
            small[i, h] = chunks[h][i]

    pl.semaphore_wait(barrier, 33)

    for part, slot in tasks:
        for (xi, zi), rows, to in obs_copies(part, slot):
            pltpu.make_async_remote_copy(
                obs.at[xi, zi, 1 - core, rows],
                to.at[:, 512:1024],
                psend_sem.at[part, slot],
                part_sem.at[part, slot],
                device_id={"tm": partner},
                device_id_type=MESH,
            ).start()

    def scatter(number, mine, gathered):
        gathered[tm] = mine[...]

        def push(step, carry):
            pltpu.make_async_remote_copy(
                mine,
                gathered.at[tm],
                esend_sem.at[number],
                erecv_sem.at[number],
                device_id={"tm": turn(tm, step, 32)},
                device_id_type=MESH,
            ).start()
            return carry

        lax.fori_loop(1, 32, push, 0)

    def gathered_wait(number, gathered):
        some = gathered.at[pl.ds(0, 31)]
        pltpu.make_async_copy(some, some, erecv_sem.at[number]).wait()

    def scattered_wait(number, gathered):
        some = gathered.at[pl.ds(0, 31)]
        pltpu.make_async_copy(some, some, esend_sem.at[number]).wait()

    scatter(0, e1, g1)

    def obs_wait(part, slot):
        to = held[part].at[slot, :, :, pl.ds(0, 512)]
        pltpu.make_async_copy(to, to, own_sem.at[part, slot]).wait()
        pltpu.make_async_copy(to, to, part_sem.at[part, slot]).wait()

    def project(part, slot):
        u = UNIT[part]

        def block(k, carry):
            if part == 0:
                left, right, to = oa[slot], bas[k], (slot * 4 + k) * 384
            elif part == 1:
                left, right, to = ob[k], bas[slot], (slot * 4 + k) * 320
            else:
                left, right, to = oc[slot], bas[k], slot * 1280 + k * 80
            total = jnp.dot(left.reshape(4 * u, 1024), right, preferred_element_type=F32)
            if part < 2:
                acc[part][pl.ds(pl.multiple_of(to, 16), 4 * u), :] = total
            else:
                for xr in range(4):
                    acc[part][pl.ds(pl.multiple_of(to + xr * 320, 16), 80), :] = total[xr * 80 : xr * 80 + 80]
            return carry

        lax.fori_loop(0, 4, block, 0)

    def place(part, stage, message):
        slot, half, _ = MESSAGES[message]
        begin, rows = half_rows(part, stage, half)
        return slot * stage_rows(part, stage) + begin, rows

    def peak(block):
        return jnp.max(jnp.abs(block).reshape(-1, 8, 256), axis=0)

    def copies(part, stage, message):
        _, _, way = MESSAGES[message]
        begin, rows = place(part, stage, message)
        to = neighbour(ORDER[part][stage], way)
        number = (part * 3 + stage) * 6 + message
        return (
            pltpu.make_async_remote_copy(
                quant[part].at[pl.ds(begin, rows)],
                landed[part][stage].at[message, pl.ds(0, rows)],
                send_sem.at[number],
                recv_sem.at[number],
                device_id=to,
                device_id_type=MESH,
            ),
            pltpu.make_async_remote_copy(
                scale_out.at[number],
                scale_in.at[number],
                ssend_sem.at[number],
                srecv_sem.at[number],
                device_id=to,
                device_id_type=MESH,
            ),
        )

    def recv_wait(part, stage, message):
        for copy in copies(part, stage, message):
            copy.wait_recv()

    def send(part, stage, message, relayed=None):
        begin, rows = place(part, stage, message)
        number = (part * 3 + stage) * 6 + message
        size = chunk_rows(part, rows)
        if relayed is not None:
            recv_wait(part, stage, relayed)
            factor = scale_in[(part * 3 + stage) * 6 + relayed]

        def measure(k, top):
            at = pl.ds(pl.multiple_of(begin + k * size, 16), size)
            block = acc[part][at, :]
            if relayed is not None:
                came = landed[part][stage][relayed, pl.ds(pl.multiple_of(k * size, 16), size), :]
                block = block + came.astype(F32) * factor
                acc[part][at, :] = block
            return jnp.maximum(top, peak(block))

        top = lax.fori_loop(0, rows // size, measure, jnp.zeros((8, 256), F32))
        top = jnp.maximum(jnp.max(top, axis=0, keepdims=True), TINY)
        scale_out[number] = top * (1.0 / LIMIT)
        inverse = LIMIT / top

        def encode(k, carry):
            at = pl.ds(pl.multiple_of(begin + k * size, 16), size)
            quant[part][at, :] = jnp.round(acc[part][at, :] * inverse).astype(I16)
            return carry

        lax.fori_loop(0, rows // size, encode, 0)
        for copy in copies(part, stage, message):
            copy.start()

    def finish(part, stage):
        for half, (left, right) in enumerate(((2, 4), (3, 5))):
            begin, rows = half_rows(part, stage, half)
            size = chunk_rows(part, rows)
            for message in (left, right):
                recv_wait(part, stage, message)
            scales = [scale_in[(part * 3 + stage) * 6 + m] for m in (left, right)]

            def add(k, carry):
                at = pl.ds(pl.multiple_of(begin + k * size, 16), size)
                block = acc[part][at, :]
                for m, factor in zip((left, right), scales):
                    came = landed[part][stage][m, pl.ds(pl.multiple_of(k * size, 16), size), :]
                    block = block + came.astype(F32) * factor
                acc[part][at, :] = block
                return carry

            lax.fori_loop(0, rows // size, add, 0)

    for yr in range(4):
        pltpu.make_async_copy(bas.at[yr], bas.at[yr], bas_sem.at[yr]).wait()
    for part in range(3):
        if part == 1:
            for slot in range(4):
                obs_wait(1, slot)
        else:
            obs_wait(part, 2)
        project(part, 2)
        send(part, 0, 0)
        send(part, 0, 1)
    for slot, message in ((1, 3), (3, 4)):
        for part in range(3):
            if part != 1:
                obs_wait(part, slot)
            project(part, slot)
            send(part, 0, message)

    gathered_wait(0, g1)

    def enter(k, v):
        new = []
        for h in range(2):
            lanes = slice(h * 128, h * 128 + 128)
            lead, spread, weight = (g1[k, i : i + 1, lanes] for i in range(3))
            new.append(jnp.where(k < tm, lead * lead * v[h] / (1.0 + weight * v[h]) + spread, v[h]))
        return tuple(new)

    v = lax.fori_loop(0, 31, enter, (jnp.zeros((1, 128), F32),) * 2)
    after = turn(tm, 1, 32)
    for h in range(2):
        lanes = slice(h * 128, h * 128 + 128)
        dec[h, 256:257, :] = jnp.where(tm == 31, 0.0, g1[after, 3:4, lanes])
        now = v[h]
        for k in range(8):
            small[3, h, k : k + 1, :] = now
            lead, spread, weight = (small[i, h, k : k + 1, :] for i in range(3))
            now = lead * lead * now / (1.0 + weight * now) + spread

    def forward(s, carry):
        seen = flag[steps(s), :]
        out = []
        for h in range(2):
            v, prefix = carry[h]
            d, q = dec[h, steps(s), :], qv[h, steps(s), :]
            vp = d * d * v + q
            den = 1.0 / (vp + noise[h])
            retain = (noise[h] + (1.0 - seen) * vp) * den
            v = retain * vp
            a = retain * d
            prefix = prefix * a
            vv[h, steps(s), :] = v
            aa[h, steps(s), :] = a
            kk[h, steps(s), :] = seen * vp * den
            ap[h, steps(s), :] = prefix
            out.append((v, prefix))
        return tuple(out)

    ends = lax.fori_loop(0, 32, forward, tuple((small[3, h], one) for h in range(2)))

    def backward(i, carry):
        s = 31 - i
        out = []
        for h in range(2):
            var, pull, suffix = carry[h]
            nd, v = dec[h, steps(s + 1), :], vv[h, steps(s), :]
            inverse = 1.0 / (nd * nd * v + process[h])
            g, w = v * nd * inverse, process[h] * inverse
            var = g * g * var + v * w
            pull = g * pull + w * ap[h, steps(s), :]
            suffix = g * suffix
            gg[h, steps(s), :] = g
            ww[h, steps(s), :] = w
            sv[h, steps(s), :] = var
            sm[h, steps(s), :] = pull
            gs[h, steps(s), :] = suffix
            out.append((var, pull, suffix))
        return tuple(out)

    heads = lax.fori_loop(0, 32, backward, ((nil, nil, one), (nil, nil, one)))
    for h in range(2):
        lanes = slice(h * 128, h * 128 + 128)
        var, pull, suffix = heads[h]
        last = ends[h][1]
        small[4, h], small[5, h], small[6, h] = last, pull, suffix
        small[7, h] = var
        m = jnp.ones((1, 128), F32)
        starts = []
        for k in range(8):
            starts.append(m)
            m = m * last[k : k + 1]
        e2[0:1, lanes] = m
        s_var, s_pull, s_suffix = jnp.zeros((1, 128), F32), jnp.zeros((1, 128), F32), jnp.ones((1, 128), F32)
        for k in range(7, -1, -1):
            g = suffix[k : k + 1]
            s_var = var[k : k + 1] + g * g * s_var
            s_pull = pull[k : k + 1] * starts[k] + g * s_pull
            s_suffix = g * s_suffix
        e2[1:2, lanes], e2[2:3, lanes], e2[3:4, lanes] = s_pull, s_suffix, s_var
    scatter(1, e2, g2)

    for part in range(3):
        send(part, 0, 2, relayed=0)
        send(part, 0, 5, relayed=1)
    for part in range(3):
        if part != 1:
            obs_wait(part, 0)
        project(part, 0)

    gathered_wait(1, g2)

    def leave(i, v):
        k = 31 - i
        new = []
        for h in range(2):
            lanes = slice(h * 128, h * 128 + 128)
            suffix, var = g2[k, 2:3, lanes], g2[k, 3:4, lanes]
            new.append(jnp.where(k > tm, var + suffix * suffix * v[h], v[h]))
        return tuple(new)

    v = lax.fori_loop(0, 31, leave, (jnp.zeros((1, 128), F32),) * 2)
    for h in range(2):
        lanes = slice(h * 128, h * 128 + 128)
        now = v[h]
        for k in range(7, -1, -1):
            rows = slice(k * 32, k * 32 + 32)
            g = gs[h, rows, :]
            lv_out[rows, lanes] = jnp.log(sv[h, rows, :] + g * g * now)
            g = small[6, h, k : k + 1, :]
            now = small[7, h, k : k + 1, :] + g * g * now

    for stage in range(3):
        for part in range(3):
            finish(part, stage)
            if stage < 2:
                for message in (0, 1, 3, 4):
                    send(part, stage + 1, message)
        if stage < 2:
            for part in range(3):
                send(part, stage + 1, 2, relayed=0)
                send(part, stage + 1, 5, relayed=1)

    for part in range(3):
        rows = slice(START[part], START[part] + UNIT[part])
        block = acc[part][0 : UNIT[part], :]
        coef_out[rows, :] = block
        for h in range(2):
            cc[h, rows, :] = block[:, h * 128 : h * 128 + 128] * kk[h, rows, :]
    for h in range(2):
        lanes = slice(h * 128, h * 128 + 128)
        pv, r = pv_ref[:, lanes], r_ref[:, lanes]
        retain = (r + (1.0 - flag[0:1, :]) * pv) / (pv + r)
        cc[h, 0:1, :] = cc[h, 0:1, :] + jnp.where(first, retain * pm_ref[:, lanes], 0.0)

    def mean_forward(s, carry):
        out = []
        for h in range(2):
            m = aa[h, steps(s), :] * carry[h] + cc[h, steps(s), :]
            ll[h, steps(s), :] = m
            out.append(m)
        return tuple(out)

    tails = lax.fori_loop(0, 32, mean_forward, (nil, nil))

    def mean_backward(i, carry):
        s = 31 - i
        out = []
        for h in range(2):
            m = gg[h, steps(s), :] * carry[h] + ww[h, steps(s), :] * ll[h, steps(s), :]
            s0[h, steps(s), :] = m
            out.append(m)
        return tuple(out)

    fronts = lax.fori_loop(0, 32, mean_backward, (nil, nil))

    def chain(h, m, s):
        into, back = [], [None] * 8
        for k in range(8):
            into.append(m)
            m = small[4, h, k : k + 1, :] * m + tails[h][k : k + 1]
        for k in range(7, -1, -1):
            back[k] = s
            s = fronts[h][k : k + 1] + small[5, h, k : k + 1, :] * into[k] + small[6, h, k : k + 1, :] * s
        return into, back, m, s

    zero = jnp.zeros((1, 128), F32)
    for h in range(2):
        lanes = slice(h * 128, h * 128 + 128)
        _, _, m, s = chain(h, zero, zero)
        e3[0:1, lanes], e3[1:2, lanes] = m, s
    scatter(2, e3, g3)
    gathered_wait(2, g3)

    def means(k, m):
        mi[k] = m
        return g2[k, 0:1, :] * m + g3[k, 0:1, :]

    lax.fori_loop(0, 32, means, jnp.zeros((1, 256), F32))

    def smooths(i, s):
        k = 31 - i
        new = g3[k, 1:2, :] + g2[k, 1:2, :] * mi[k] + g2[k, 2:3, :] * s
        return jnp.where(k > tm, new, s)

    s_in = lax.fori_loop(0, 31, smooths, jnp.zeros((1, 256), F32))
    m_in = mi[tm]
    for h in range(2):
        lanes = slice(h * 128, h * 128 + 128)
        into, back, _, _ = chain(h, m_in[:, lanes], s_in[:, lanes])
        for k in range(8):
            rows = slice(k * 32, k * 32 + 32)
            fm_out[rows, lanes] = ll[h, rows, :] + ap[h, rows, :] * into[k]
            sm_out[rows, lanes] = s0[h, rows, :] + sm[h, rows, :] * into[k] + gs[h, rows, :] * back[k]

    for part, slot in tasks:
        to = held[part].at[slot, :, :, pl.ds(0, 512)]
        pltpu.make_async_copy(to, to, psend_sem.at[part, slot]).wait()
    for part in range(3):
        for stage in range(3):
            for message in range(6):
                for copy in copies(part, stage, message):
                    copy.wait_send()
    scattered_wait(0, g1)
    scattered_wait(1, g2)
    scattered_wait(2, g3)


def body(observations, pod_basis, decay, step_mask, process_var, obs_var, prior_mean, prior_var):
    block = (256, 256)
    vmem = pl.BlockSpec(memory_space=pltpu.VMEM)
    anywhere = pl.BlockSpec(memory_space=pl.ANY)
    plane = pltpu.VMEM((2, 256, 128), F32)
    landing = [
        pltpu.VMEM((6, half_rows(p, s, 0)[1], 256), I16) for p in range(3) for s in range(3)
    ]
    dma = pltpu.SemaphoreType.DMA
    scratch = [
        *[pltpu.VMEM((rows, 256), F32) for rows in ROWS],
        *[pltpu.VMEM((rows, 256), I16) for rows in ROWS],
        *landing,
        *[pltpu.VMEM((4, 4, u, 1024), BF16) for u in UNIT],
        pltpu.VMEM((4, 1024, 256), BF16),
        pltpu.VMEM((54, 1, 256), F32),
        pltpu.VMEM((54, 1, 256), F32),
        pltpu.VMEM((2, 264 + 24, 128), F32),
        pltpu.VMEM((256, 128), F32),
        *[plane] * 13,
        pltpu.VMEM((8, 2, 8, 128), F32),
        pltpu.VMEM((4, 256), F32),
        pltpu.VMEM((4, 256), F32),
        pltpu.VMEM((2, 256), F32),
        pltpu.VMEM((32, 4, 256), F32),
        pltpu.VMEM((32, 4, 256), F32),
        pltpu.VMEM((32, 2, 256), F32),
        pltpu.VMEM((32, 1, 256), F32),
        dma((3, 4)),
        dma((3, 4)),
        dma((3, 4)),
        dma((4,)),
        dma((54,)),
        dma((54,)),
        dma((54,)),
        dma((54,)),
        dma((3,)),
        dma((3,)),
    ]
    return tuple(
        pl.pallas_call(
            kernel,
            out_shape=[jax.ShapeDtypeStruct(block, F32)] * 4,
            in_specs=[anywhere, anywhere, *[vmem] * 6],
            out_specs=[vmem] * 4,
            scratch_shapes=scratch,
            compiler_params=pltpu.CompilerParams(
                collective_id=0, has_side_effects=True, vmem_limit_bytes=60 * 2**20
            ),
        )(
            observations.reshape(4, 4, 2, 256, 512),
            pod_basis.reshape(32, 512, 1024),
            decay,
            step_mask.reshape(1, 256),
            process_var.reshape(1, 256),
            obs_var.reshape(1, 256),
            prior_mean.reshape(1, 256),
            prior_var.reshape(1, 256),
        )
    )


def solution(mesh):
    return jax.shard_map(
        body,
        mesh=mesh,
        in_specs=(
            P(None, "tm", "space", None),
            P(None, "space", None, None),
            P("tm", "space"),
            P("tm"),
            P("space"),
            P("space"),
            P("space"),
            P("space"),
        ),
        out_specs=(P("tm", "space"), P("tm", "space"), P("tm", "space"), P("tm", "space")),
        check_vma=False,
    )
```

time: 1010 us -> 81 us (0.08)
  waiting for transfers between devices: 692 us -> 0 us
  blocking collectives: 193 us -> 0 us
  Pallas kernels: 0 us -> 73.5 us
  local copies, waits for them, and re-layouts: 49.7 us -> 6.68 us
  other arithmetic: 32.9 us -> 0 us
  matrix products: 18.7 us -> 0 us
  between operations: 16.8 us -> 0.64 us
    reduce_scatter x1 -> x0, waiting for transfers between devices: 692 us -> none  [body(): lax.psum_scatter(terms, ('tm', 'space'), scatter_dimension=0, tiled=True)[0]]
    all_gather x8 -> x0, blocking collectives: 193 us -> none  [entering(): pieces = jax.tree.map(lambda part: lax.all_gather(part, axis), value)]
    pallas_call x0 -> x1, Pallas kernels: none -> 73.5 us  [body(): pl.pallas_call(kernel, out_shape=[jax.ShapeDtypeStruct(block, F32)] * 4,...]
    transpose x1 -> x0, local copies, waits for them, and re-layouts: 33.4 us -> none  [body(): jnp.einsum('tsc,cnk->tnsk', own_slab, own_basis, preferred_element_type=j...]
    select_n x62 -> x0, other arithmetic: 21.8 us -> none  [turn(): jnp.where(position < mine, new, old)]
    dot_general x1 -> x0, matrix products: 18.7 us -> none  [body(): jnp.einsum('tsc,cnk->tnsk', own_slab, own_basis, preferred_element_type=j...]
    slice x220 -> x0, local copies, waits for them, and re-layouts: 10.3 us -> none  [the longest x131 6.92 us: body(): local_prefix = lax.associative_scan(filter_combine, elements, axis=0)]
  transfers between devices with their start and end apart: 2 -> 0, of which waited for: 1 -> 0; matrix products, arithmetic and copies ran while one was open for 4% -> 0% of each run, Pallas kernels for 0% -> 0%
where the time goes in v1:
time: 81 us; the launch traced here: 80.8 us
  Pallas kernels  73.5 us (91%)
  local copies, waits for them, and re-layouts  6.68 us (8%)
    pallas_call x1, Pallas kernels, body(): pl.pallas_call(kernel, out_shape=[jax.ShapeDtypeStruct(block, F32)] * 4,...  73.5 us
    unnamed x4, local copies, waits for them, and re-layouts  6.68 us

profile of v1, /device:TPU:1, one launch (start us, length us, event | category | flops | bytes accessed | tf_op | source)
XLA Modules:
  0.0 80.8 jit_solution(4775567845538044786)
XLA Ops:
  0.6 73.5 %shard_map.111 = (f32[256,256]{1,0:T(8,128)}, f32[256,256]{1,0:T(8,128)}, f32[256,256]{1,0:T(8,128)}, f32[256,256]{1,0:T(8,128)}) custom-call(bf16[4,4,2,256,512]{4,3,2,1,0:T(8,128)(2,1)} %bitcast.8, bf16[32,512,1024]{2,1,0:T(8,128)(2,1)} %bitcast.7, f32[256,256]{1,0:T(8,128)} %decay.1, s32[1,256]{1,0:T(1,128)} %bitcast.9, f32[1,256]{1,0:T(1,128)} %bitcast.10, ...), custom_call_target="tpu_custom_call" | custom-call | tf_op jit(solution)/shard_map/pallas_call | solution.py:562
  74.1 1.7 %copy.16 = f32[256,256]{1,0:T(8,128)} copy(f32[256,256]{1,0:T(8,128)} %get-tuple-element.8) | data formatting | bytes 524288
  75.8 1.7 %copy.17 = f32[256,256]{1,0:T(8,128)} copy(f32[256,256]{1,0:T(8,128)} %get-tuple-element.9) | data formatting | bytes 524288
  77.4 1.7 %copy.18 = f32[256,256]{1,0:T(8,128)} copy(f32[256,256]{1,0:T(8,128)} %get-tuple-element.10) | data formatting | bytes 524288
  79.1 1.7 %copy.19 = f32[256,256]{1,0:T(8,128)} copy(f32[256,256]{1,0:T(8,128)} %get-tuple-element.11) | data formatting | bytes 524288

commit v2 on v0

v2 whole, which is shorter than its diff:
```python
import jax
import jax.numpy as jnp
from jax import lax
from jax.experimental import pallas as pl
from jax.experimental.pallas import tpu as pltpu
from jax.sharding import PartitionSpec as P

MESH = pl.DeviceIdType.MESH
F32 = jnp.float32
BF16 = jnp.bfloat16
I16 = jnp.int16

UNIT = (96, 64, 96)
START = (0, 96, 160)
ORDER = (("x", "y", "z"), ("y", "z", "x"), ("z", "y", "x"))
ROWS = tuple(64 * u for u in UNIT)
LIMIT = 32760.0
TINY = 1e-33
TURNS = (0, 2, 1)

MESSAGES = ((2, 0, 1), (2, 1, -1), (1, 0, 1), (1, 1, 1), (3, 0, -1), (3, 1, -1))


def turn(value, by, count):
    return lax.rem(value + by, count)


def sub_block(i):
    return lax.rem(2 + 3 * i + 3 * (i // 2) + 2 * (i // 3), 4)


def lane(h):
    return slice(h * 128, h * 128 + 128)


def kernel(obs, basis, decay, mask, q_ref, r_ref, pm_ref, pv_ref, *refs):
    outs, scratch = refs[:8], refs[8:]
    (made, last, made_sem, fa, fb, fc, qa, qb, qc, ra1, ra2, ra3, rb1, rb2, rb3, rc1, rc2, rc3, oa, ob, oc, bas, scale_out, scale_in,
     dec, flag, qv, vv, aa, kk, gg, ww, ap, sm, gs, sv, cc, ll, s0, small, e1, e2, e3, g1, g2, g3, wm, ws, wl,
     own_sem, part_sem, psend_sem, bas_sem, send_sem, recv_sem, ssend_sem, srecv_sem, esend_sem, erecv_sem) = scratch
    def put(i):
        source = last if i == 7 else made.at[i]
        return pltpu.make_async_copy(source, outs[i], made_sem.at[i])

    acc = (fa, fb, fc)
    quant = (qa, qb, qc)
    landed = ((ra1, ra2, ra3), (rb1, rb2, rb3), (rc1, rc2, rc3))
    held = (oa, ob, oc)
    tm = lax.axis_index("tm")
    y = lax.axis_index("space")
    x, z, core = tm // 8, lax.rem(tm // 2, 4), lax.rem(tm, 2)
    partner = tm + 1 - 2 * core

    def neighbour(axis, way):
        if axis == "x":
            return {"tm": turn(tm, 8 if way > 0 else 24, 32)}
        if axis == "z":
            return {"tm": x * 8 + turn(z, 1 if way > 0 else 3, 4) * 2 + core}
        return {"space": turn(y, 1 if way > 0 else 3, 4)}

    barrier = pltpu.get_barrier_semaphore()

    def greet(step, carry):
        pl.semaphore_signal(barrier, inc=1, device_id={"tm": turn(tm, step, 32)}, device_id_type=MESH)
        return carry

    lax.fori_loop(1, 32, greet, 0)
    for way in (1, -1):
        pl.semaphore_signal(barrier, inc=1, device_id=neighbour("y", way), device_id_type=MESH)

    def obs_copies(part, slot):
        rows = slice(START[part], START[part] + UNIT[part])
        pieces = []
        for other in range(4):
            at = (turn(x, slot, 4), turn(z, other, 4)) if part == 0 else (turn(x, other, 4), turn(z, slot, 4))
            pieces.append((at, rows, held[part].at[slot, other]))
        return pieces

    tasks = [(0, 2), (2, 2), (1, 2), (1, 1), (1, 3), (1, 0), (0, 1), (0, 3), (0, 0), (2, 1), (2, 3), (2, 0)]
    for yr in (2, 1, 3, 0):
        columns = pl.ds(pl.multiple_of(turn(y, yr, 4) * 256, 256), 256)
        for side, who in ((0, tm), (1, partner)):
            pltpu.make_async_copy(
                basis.at[who, :, columns], bas.at[yr, pl.ds(side * 512, 512)], bas_sem.at[yr]
            ).start()
    for part, slot in tasks:
        for (xi, zi), rows, to in obs_copies(part, slot):
            pltpu.make_async_copy(obs.at[xi, zi, core, rows], to.at[:, 0:512], own_sem.at[part, slot]).start()

    first = tm == 0
    for h in range(2):
        dec[h, 0:256, :] = decay[:, lane(h)]
        e1[3:4, lane(h)] = dec[h, 0:1, :]
        qv[h] = jnp.broadcast_to(q_ref[:, lane(h)], (256, 128))
        qv[h, 0:1, :] = jnp.where(first, pv_ref[:, lane(h)], q_ref[:, lane(h)])
        dec[h, 0:1, :] = jnp.where(first, 0.0, dec[h, 0:1, :])
    row = lax.broadcasted_iota(jnp.int32, (256, 256), 0)
    column = lax.broadcasted_iota(jnp.int32, (256, 256), 1)
    spread_mask = jnp.where(row == column, jnp.broadcast_to(mask[...].astype(F32), (256, 256)), 0.0).astype(BF16)
    flag[...] = jnp.dot(spread_mask, jnp.ones((256, 128), BF16), preferred_element_type=F32)

    def wide(ref, h):
        return jnp.broadcast_to(ref[:, lane(h)], (8, 128))

    blocks = [(g, h) for g in range(2) for h in range(2)]

    def steps(s, g):
        return pl.ds(g * 128 + s, 8, stride=16)

    def join(early, late):
        lead_e, spread_e, weight_e = early
        lead_l, spread_l, weight_l = late
        factor = 1.0 / (1.0 + spread_e * weight_l)
        return (
            lead_l * factor * lead_e,
            lead_l * lead_l * factor * spread_e + spread_l,
            lead_e * lead_e * factor * weight_l + weight_e,
        )

    def compose(s, carry):
        out = []
        for (g, h), early in zip(blocks, carry):
            seen, d, q = flag[steps(s, g), :], dec[h, steps(s, g), :], qv[h, steps(s, g), :]
            noise = wide(r_ref, h)
            den = 1.0 / (q + noise)
            retain = (noise + (1.0 - seen) * q) * den
            out.append(join(early, (retain * d, retain * q, seen * d * d * den)))
        return tuple(out)

    one, nil = jnp.ones((8, 128), F32), jnp.zeros((8, 128), F32)
    unit, zero = jnp.ones((1, 128), F32), jnp.zeros((1, 128), F32)
    chunks = lax.fori_loop(0, 16, compose, ((one, nil, nil),) * 4, unroll=2)
    totals = []
    for (g, h), parts in zip(blocks, chunks):
        for i in range(3):
            small[i, h, g * 8 : g * 8 + 8, :] = parts[i]
        totals.append(tuple(part[0:1] for part in parts))
    for k in range(1, 8):
        totals = [join(t, tuple(p[k : k + 1] for p in parts)) for t, parts in zip(totals, chunks)]
    for h in range(2):
        for i, value in enumerate(join(totals[h], totals[2 + h])):
            e1[i : i + 1, lane(h)] = value
        for i in range(3):
            small[11 + i, h, 0:1, :] = totals[h][i]

    pl.semaphore_wait(barrier, 33)

    for part, slot in tasks:
        for (xi, zi), rows, to in obs_copies(part, slot):
            pltpu.make_async_remote_copy(
                obs.at[xi, zi, 1 - core, rows],
                to.at[:, 512:1024],
                psend_sem.at[part, slot],
                part_sem.at[part, slot],
                device_id={"tm": partner},
                device_id_type=MESH,
            ).start()

    def scatter(number, mine, gathered):
        gathered[tm] = mine[...]

        def push(step, carry):
            pltpu.make_async_remote_copy(
                mine,
                gathered.at[tm],
                esend_sem.at[number],
                erecv_sem.at[number],
                device_id={"tm": turn(tm, step, 32)},
                device_id_type=MESH,
            ).start()
            return carry

        lax.fori_loop(1, 32, push, 0)

    def gathered_wait(number, gathered, sem):
        some = gathered.at[pl.ds(0, 31)]
        pltpu.make_async_copy(some, some, sem.at[number]).wait()

    scatter(0, e1, g1)

    def obs_wait(part, slot):
        to = held[part].at[slot, :, :, pl.ds(0, 512)]
        pltpu.make_async_copy(to, to, own_sem.at[part, slot]).wait()
        pltpu.make_async_copy(to, to, part_sem.at[part, slot]).wait()

    def product(part, slot, j):
        u = UNIT[part]
        obs_slot, mode_slot = (j, slot) if part == 1 else (slot, j)
        return jnp.dot(held[part][obs_slot].reshape(4 * u, 1024), bas[mode_slot], preferred_element_type=F32)

    def place(part, stage, message, j):
        slot, half, _ = MESSAGES[message]
        u = UNIT[part]
        if stage == 0:
            return (slot * 4 + j) * (4 * u) + half * (2 * u), 2 * u
        if stage == 1:
            return slot * 4 * u + half * 2 * u, 2 * u
        return slot * u + half * (u // 2), u // 2

    def number_of(part, stage, message, j):
        return part * 36 + (j * 6 if stage == 0 else 18 + 6 * stage) + message

    def index_of(stage, message, j):
        return j * 6 + message if stage == 0 else message

    def peak(block):
        return jnp.max(jnp.abs(block).reshape(-1, 8, 256), axis=0)

    def steps_of(top):
        top = jnp.maximum(jnp.max(top, axis=0, keepdims=True), TINY)
        return top * (1.0 / LIMIT), LIMIT / top

    def copies(part, stage, message, j):
        begin, rows = place(part, stage, message, j)
        to = neighbour(ORDER[part][stage], MESSAGES[message][2])
        number = number_of(part, stage, message, j)
        return (
            pltpu.make_async_remote_copy(
                quant[part].at[pl.ds(pl.multiple_of(begin, 16), rows)],
                landed[part][stage].at[index_of(stage, message, j)],
                send_sem.at[part, stage],
                recv_sem.at[number],
                device_id=to,
                device_id_type=MESH,
            ),
            pltpu.make_async_remote_copy(
                scale_out.at[number],
                scale_in.at[number],
                ssend_sem.at[part, stage],
                srecv_sem.at[number],
                device_id=to,
                device_id_type=MESH,
            ),
        )

    def recv_wait(part, stage, message, j):
        for copy in copies(part, stage, message, j):
            copy.wait_recv()

    def send(part, stage, message, j=0, relayed=None):
        begin, rows = place(part, stage, message, j)
        number = number_of(part, stage, message, j)
        size = min(rows, 64)
        if relayed is not None:
            recv_wait(part, stage, relayed, j)
            factor = scale_in[number_of(part, stage, relayed, j)]

        def measure(k, top):
            at = pl.ds(pl.multiple_of(begin + k * size, 16), size)
            block = acc[part][at, :]
            if relayed is not None:
                came = landed[part][stage][index_of(stage, relayed, j), pl.ds(pl.multiple_of(k * size, 16), size), :]
                block = block + came.astype(F32) * factor
                acc[part][at, :] = block
            return jnp.maximum(top, peak(block))

        top = lax.fori_loop(0, rows // size, measure, jnp.zeros((8, 256), F32))
        scale_out[number], inverse = steps_of(top)

        def encode(k, carry):
            at = pl.ds(pl.multiple_of(begin + k * size, 16), size)
            quant[part][at, :] = jnp.round(acc[part][at, :] * inverse).astype(I16)
            return carry

        lax.fori_loop(0, rows // size, encode, 0)
        for copy in copies(part, stage, message, j):
            copy.start()

    def far(part, j):
        total = product(part, 2, j)
        u = UNIT[part]
        for message in (0, 1):
            begin, rows = place(part, 0, message, j)
            block = total[message * 2 * u : message * 2 * u + 2 * u]
            scale_out[number_of(part, 0, message, j)], inverse = steps_of(peak(block))
            at = pl.ds(pl.multiple_of(begin, 16), rows)
            quant[part][at, :] = jnp.round(block * inverse).astype(I16)
            for copy in copies(part, 0, message, j):
                copy.start()

    def rest(part, j):
        u = UNIT[part]

        def block(k, carry):
            slot = lax.rem(1 + 2 * k + 3 * (k // 2), 4)
            acc[part][pl.ds(pl.multiple_of((slot * 4 + j) * (4 * u), 16), 4 * u), :] = product(part, slot, j)
            return carry

        lax.fori_loop(0, 3, block, 0)
        send(part, 0, 3, j)
        send(part, 0, 4, j)

    def finish(part, stages, j=0):
        u = UNIT[part]
        rows = u // 2 if stages == (2,) else 2 * u
        size = min(rows, 64)
        for half, pair in enumerate(((2, 4), (3, 5))):
            begin = half * rows + (j * (4 * u) if stages == (0,) else 0)
            came = [(stage, message) for stage in stages for message in pair]
            for stage, message in came:
                recv_wait(part, stage, message, j)
            scales = [scale_in[number_of(part, stage, m, j)] for stage, m in came]

            def add(k, carry):
                at = pl.ds(pl.multiple_of(begin + k * size, 16), size)
                block = acc[part][at, :]
                for (stage, m), factor in zip(came, scales):
                    rows_in = pl.ds(pl.multiple_of(k * size, 16), size)
                    block = block + landed[part][stage][index_of(stage, m, j), rows_in, :].astype(F32) * factor
                acc[part][at, :] = block
                return carry

            lax.fori_loop(0, rows // size, add, 0)

    def variances():
        gathered_wait(0, g1, erecv_sem)

        def enter(k, v):
            lead, spread, weight = (g1[k, i : i + 1, :] for i in range(3))
            return jnp.where(k < tm, lead * lead * v / (1.0 + weight * v) + spread, v)

        v = lax.fori_loop(0, 31, enter, jnp.zeros((1, 256), F32), unroll=2)
        after = turn(tm, 1, 32)
        now = []
        for h in range(2):
            dec[h, 256:257, :] = jnp.where(tm == 31, 0.0, g1[after, 3:4, lane(h)])
            now.append(v[:, lane(h)])
        for h in range(2):
            lead, spread, weight = (small[11 + i, h, 0:1, :] for i in range(3))
            now.append(lead * lead * now[h] / (1.0 + weight * now[h]) + spread)
        for k in range(8):
            for b, (g, h) in enumerate(blocks):
                at = slice(g * 8 + k, g * 8 + k + 1)
                small[3, h, at, :] = now[b]
                if k < 7:
                    lead, spread, weight = (small[i, h, at, :] for i in range(3))
                    now[b] = lead * lead * now[b] / (1.0 + weight * now[b]) + spread

        def forward(s, carry):
            out = []
            for (g, h), (v, prefix) in zip(blocks, carry):
                seen, d, q = flag[steps(s, g), :], dec[h, steps(s, g), :], qv[h, steps(s, g), :]
                noise = wide(r_ref, h)
                vp = d * d * v + q
                den = 1.0 / (vp + noise)
                retain = (noise + (1.0 - seen) * vp) * den
                v = retain * vp
                a = retain * d
                prefix = prefix * a
                vv[h, steps(s, g), :] = v
                aa[h, steps(s, g), :] = a
                kk[h, steps(s, g), :] = seen * vp * den
                ap[h, steps(s, g), :] = prefix
                out.append((v, prefix))
            return tuple(out)

        starts = tuple((small[3, h, g * 8 : g * 8 + 8, :], one) for g, h in blocks)
        ends = lax.fori_loop(0, 16, forward, starts, unroll=2)
        for (g, h), (_, prefix) in zip(blocks, ends):
            small[4, h, g * 8 : g * 8 + 8, :] = prefix

    def smoother():
        def backward(i, carry):
            s = 15 - i
            out = []
            for (g, h), (var, pull, suffix) in zip(blocks, carry):
                nd, v = dec[h, steps(s + 1, g), :], vv[h, steps(s, g), :]
                process = wide(q_ref, h)
                inverse = 1.0 / (nd * nd * v + process)
                gain, w = v * nd * inverse, process * inverse
                var = gain * gain * var + v * w
                pull = gain * pull + w * ap[h, steps(s, g), :]
                suffix = gain * suffix
                gg[h, steps(s, g), :] = gain
                ww[h, steps(s, g), :] = w
                sv[h, steps(s, g), :] = var
                sm[h, steps(s, g), :] = pull
                gs[h, steps(s, g), :] = suffix
                out.append((var, pull, suffix))
            return tuple(out)

        heads = lax.fori_loop(0, 16, backward, ((nil, nil, one),) * 4, unroll=2)
        for (g, h), (var, pull, suffix) in zip(blocks, heads):
            rows = slice(g * 8, g * 8 + 8)
            small[5, h, rows, :], small[6, h, rows, :], small[7, h, rows, :] = pull, suffix, var
        for h in range(2):
            m = unit
            for k in range(16):
                small[8, h, k : k + 1, :] = m
                m = m * small[4, h, k : k + 1, :]
            e2[0:1, lane(h)] = m
            s_var, s_pull, s_suffix = zero, zero, unit
            for k in range(15, -1, -1):
                at = slice(k, k + 1)
                small[9, h, at, :], small[10, h, at, :] = s_pull, s_suffix
                g = small[6, h, at, :]
                s_var = small[7, h, at, :] + g * g * s_var
                s_pull = small[5, h, at, :] * small[8, h, at, :] + g * s_pull
                s_suffix = g * s_suffix
            e2[1:2, lane(h)], e2[2:3, lane(h)], e2[3:4, lane(h)] = s_pull, s_suffix, s_var
        scatter(1, e2, g2)

    def weights():
        gathered_wait(1, g2, erecv_sem)

        def down(i, carry):
            k = 31 - i
            var, w = carry
            prefix, suffix, spread = g2[k, 0:1, :], g2[k, 2:3, :], g2[k, 3:4, :]
            wm[k] = jnp.where(k < tm, w, 0.0)
            return (
                jnp.where(k > tm, spread + suffix * suffix * var, var),
                jnp.where(k < tm, prefix * w, w),
            )

        var, _ = lax.fori_loop(0, 32, down, (jnp.zeros((1, 256), F32), jnp.ones((1, 256), F32)), unroll=2)

        def up(k, w):
            ws[k] = jnp.where(k > tm, w, 0.0)
            return jnp.where(k > tm, g2[k, 2:3, :] * w, w)

        lax.fori_loop(0, 32, up, jnp.ones((1, 256), F32), unroll=2)

        def across(i, pull):
            k = 31 - i
            wl[k] = pull
            return ws[k] * g2[k, 1:2, :] + g2[k, 0:1, :] * pull

        lax.fori_loop(0, 32, across, jnp.zeros((1, 256), F32), unroll=2)
        for h in range(2):
            now = var[:, lane(h)]
            for k in range(15, -1, -1):
                rows, at = slice(k * 16, k * 16 + 16), slice(k, k + 1)
                g = gs[h, rows, :]
                prefix, pull, suffix = (small[i, h, at, :] for i in (8, 9, 10))
                made[6, rows, lane(h)] = jnp.log(sv[h, rows, :] + g * g * now)
                made[2, rows, lane(h)] = ap[h, rows, :] * prefix
                made[4, rows, lane(h)] = sm[h, rows, :] * prefix + g * pull
                made[5, rows, lane(h)] = g * suffix
                g = small[6, h, at, :]
                now = small[7, h, at, :] + g * g * now
        for i in (2, 4, 5, 6):
            put(i).start()

    for yr in range(4):
        pltpu.make_async_copy(bas.at[yr], bas.at[yr], bas_sem.at[yr]).wait()

    obs_wait(0, 2)
    obs_wait(2, 2)

    def farthest(i, carry):
        j = sub_block(i)
        far(0, j)
        far(2, j)
        obs_wait(1, j)
        far(1, j)
        return carry

    lax.fori_loop(0, 4, farthest, 0)
    for part in (0, 2):
        for slot in (1, 3, 0):
            obs_wait(part, slot)

    def round_of(i, carry):
        @pl.when(i < 4)
        def _():
            j = sub_block(i)
            for part in TURNS:
                rest(part, j)
            for part in TURNS:
                send(part, 0, 2, j, relayed=0)
                send(part, 0, 5, j, relayed=1)

        pl.when(i == 0)(variances)
        pl.when(i == 1)(smoother)
        pl.when(i == 2)(weights)

        @pl.when((i >= 1) & (i < 4))
        def _():
            j = sub_block(i - 1)
            for part in TURNS:
                finish(part, (0,), j)

                @pl.when(i == 1)
                def _():
                    send(part, 1, 0)
                    send(part, 1, 1)

                @pl.when(i == 2)
                def _():
                    send(part, 1, 3)
                    send(part, 1, 2, relayed=0)

                @pl.when(i == 3)
                def _():
                    send(part, 1, 4)
                    send(part, 1, 5, relayed=1)

        return carry

    lax.fori_loop(0, 4, round_of, 0)

    for part in TURNS:
        finish(part, (0, 1))
        for message in (0, 1, 3, 4):
            send(part, 2, message)
    for part in TURNS:
        send(part, 2, 2, relayed=0)
        send(part, 2, 5, relayed=1)
    for part in TURNS:
        finish(part, (2,))
        rows = slice(START[part], START[part] + UNIT[part])
        block = acc[part][0 : UNIT[part], :]
        made[0, rows, :] = block
        for h in range(2):
            cc[h, rows, :] = block[:, lane(h)] * kk[h, rows, :]
    put(0).start()

    for h in range(2):
        pv, r = pv_ref[:, lane(h)], r_ref[:, lane(h)]
        retain = (r + (1.0 - flag[0:1, :]) * pv) / (pv + r)
        cc[h, 0:1, :] = cc[h, 0:1, :] + jnp.where(first, retain * pm_ref[:, lane(h)], 0.0)

    def mean_forward(s, carry):
        out = []
        for (g, h), m in zip(blocks, carry):
            m = aa[h, steps(s, g), :] * m + cc[h, steps(s, g), :]
            ll[h, steps(s, g), :] = m
            out.append(m)
        return tuple(out)

    tails = lax.fori_loop(0, 16, mean_forward, (nil,) * 4, unroll=4)

    def mean_backward(i, carry):
        s = 15 - i
        out = []
        for (g, h), m in zip(blocks, carry):
            m = gg[h, steps(s, g), :] * m + ww[h, steps(s, g), :] * ll[h, steps(s, g), :]
            s0[h, steps(s, g), :] = m
            out.append(m)
        return tuple(out)

    fronts = lax.fori_loop(0, 16, mean_backward, (nil,) * 4, unroll=4)
    into, back = ([None] * 16, [None] * 16), ([None] * 16, [None] * 16)
    for h in range(2):
        m, s = zero, zero
        for k in range(16):
            into[h][k] = m
            m = small[4, h, k : k + 1, :] * m + tails[k // 8 * 2 + h][k % 8 : k % 8 + 1]
        for k in range(15, -1, -1):
            back[h][k] = s
            front = fronts[k // 8 * 2 + h][k % 8 : k % 8 + 1]
            s = front + small[5, h, k : k + 1, :] * into[h][k] + small[6, h, k : k + 1, :] * s
        e3[0:1, lane(h)], e3[1:2, lane(h)] = m, s
    scatter(2, e3, g3)
    for h in range(2):
        for k in range(16):
            rows = slice(k * 16, k * 16 + 16)
            made[1, rows, lane(h)] = ll[h, rows, :] + ap[h, rows, :] * into[h][k]
            made[3, rows, lane(h)] = s0[h, rows, :] + sm[h, rows, :] * into[h][k] + gs[h, rows, :] * back[h][k]
    put(1).start()
    put(3).start()
    for part in range(3):
        u = UNIT[part]
        for stage, (begin, rows, base, count) in enumerate(
            ((16 * u, 48 * u, 0, 24), (4 * u, 12 * u, 24, 6), (u, 3 * u, 30, 6))
        ):
            some = quant[part].at[pl.ds(begin, rows)]
            pltpu.make_async_copy(some, some, send_sem.at[part, stage]).wait()
            some = scale_out.at[pl.ds(part * 36 + base, count)]
            pltpu.make_async_copy(some, some, ssend_sem.at[part, stage]).wait()
    for part, slot in tasks:
        to = held[part].at[slot, :, :, pl.ds(0, 512)]
        pltpu.make_async_copy(to, to, psend_sem.at[part, slot]).wait()
    gathered_wait(0, g1, esend_sem)
    gathered_wait(1, g2, esend_sem)
    gathered_wait(2, g3, esend_sem)
    gathered_wait(2, g3, erecv_sem)
    m_in, s_in = [jnp.zeros((1, 256), F32)] * 4, [jnp.zeros((1, 256), F32)] * 4
    for k in range(32):
        left, right = g3[k, 0:1, :], g3[k, 1:2, :]
        m_in[k % 4] = m_in[k % 4] + wm[k] * left
        s_in[k % 4] = s_in[k % 4] + (ws[k] * right + wl[k] * left)
    last[0:1, :] = (m_in[0] + m_in[1]) + (m_in[2] + m_in[3])
    last[1:2, :] = (s_in[0] + s_in[1]) + (s_in[2] + s_in[3])
    put(7).start()
    for i in range(8):
        put(i).wait()


def apply_starts(*refs):
    ins, outs, (got, start, into, back, in_sem, out_sem) = refs[:8], refs[8:12], refs[12:]

    def take(i):
        return pltpu.make_async_copy(ins[i], start if i == 7 else got.at[i], in_sem.at[i])

    def give(i):
        source = (got.at[0], into, back, got.at[6])[i]
        return pltpu.make_async_copy(source, outs[i], out_sem.at[i])

    order = (7, 1, 2, 3, 4, 5, 0, 6)
    for i in order:
        take(i).start()
    for i in (7, 1, 2):
        take(i).wait()
    m_in, s_in = start[0:1, :], start[1:2, :]
    into[...] = got[1] + got[2] * m_in
    give(1).start()
    for i in (3, 4, 5):
        take(i).wait()
    back[...] = got[3] + got[4] * m_in + got[5] * s_in
    give(2).start()
    take(0).wait()
    give(0).start()
    take(6).wait()
    give(3).start()
    for i in range(4):
        give(i).wait()


def body(observations, pod_basis, decay, step_mask, process_var, obs_var, prior_mean, prior_var):
    block = jax.ShapeDtypeStruct((256, 256), F32)
    vmem = pl.BlockSpec(memory_space=pltpu.VMEM)
    anywhere = pl.BlockSpec(memory_space=pl.ANY)
    plane = pltpu.VMEM((2, 256, 128), F32)
    landing = [
        pltpu.VMEM(shape, I16) for u in UNIT for shape in ((24, 2 * u, 256), (6, 2 * u, 256), (6, u // 2, 256))
    ]
    dma = pltpu.SemaphoreType.DMA
    scratch = [
        pltpu.VMEM((7, 256, 256), F32),
        pltpu.VMEM((2, 256), F32),
        dma((8,)),
        *[pltpu.VMEM((rows, 256), F32) for rows in ROWS],
        *[pltpu.VMEM((rows, 256), I16) for rows in ROWS],
        *landing,
        *[pltpu.VMEM((4, 4, u, 1024), BF16) for u in UNIT],
        pltpu.VMEM((4, 1024, 256), BF16),
        pltpu.VMEM((108, 1, 256), F32),
        pltpu.VMEM((108, 1, 256), F32),
        pltpu.VMEM((2, 288, 128), F32),
        pltpu.VMEM((256, 128), F32),
        *[plane] * 13,
        pltpu.VMEM((14, 2, 16, 128), F32),
        pltpu.VMEM((4, 256), F32),
        pltpu.VMEM((4, 256), F32),
        pltpu.VMEM((2, 256), F32),
        pltpu.VMEM((32, 4, 256), F32),
        pltpu.VMEM((32, 4, 256), F32),
        pltpu.VMEM((32, 2, 256), F32),
        *[pltpu.VMEM((32, 1, 256), F32)] * 3,
        dma((3, 4)),
        dma((3, 4)),
        dma((3, 4)),
        dma((4,)),
        dma((3, 3)),
        dma((108,)),
        dma((3, 3)),
        dma((108,)),
        dma((3,)),
        dma((3,)),
    ]
    made = pl.pallas_call(
        kernel,
        out_shape=[block] * 7 + [jax.ShapeDtypeStruct((2, 256), F32)],
        in_specs=[anywhere, anywhere, *[vmem] * 6],
        out_specs=[anywhere] * 8,
        scratch_shapes=scratch,
        compiler_params=pltpu.CompilerParams(
            collective_id=0, has_side_effects=True, vmem_limit_bytes=60 * 2**20
        ),
    )(
        observations.reshape(4, 4, 2, 256, 512),
        pod_basis.reshape(32, 512, 1024),
        decay,
        step_mask.reshape(1, 256),
        process_var.reshape(1, 256),
        obs_var.reshape(1, 256),
        prior_mean.reshape(1, 256),
        prior_var.reshape(1, 256),
    )
    return tuple(
        pl.pallas_call(
            apply_starts,
            out_shape=[block] * 4,
            in_specs=[anywhere] * 8,
            out_specs=[anywhere] * 4,
            scratch_shapes=[
                pltpu.VMEM((7, 256, 256), F32),
                pltpu.VMEM((2, 256), F32),
                pltpu.VMEM((256, 256), F32),
                pltpu.VMEM((256, 256), F32),
                dma((8,)),
                dma((4,)),
            ],
            compiler_params=pltpu.CompilerParams(vmem_limit_bytes=60 * 2**20),
        )(*made)
    )


def solution(mesh):
    return jax.shard_map(
        body,
        mesh=mesh,
        in_specs=(
            P(None, "tm", "space", None),
            P(None, "space", None, None),
            P("tm", "space"),
            P("tm"),
            P("space"),
            P("space"),
            P("space"),
            P("space"),
        ),
        out_specs=(P("tm", "space"), P("tm", "space"), P("tm", "space"), P("tm", "space")),
        check_vma=False,
    )
```

time: 1010 us -> 72.7 us (0.07)
  waiting for transfers between devices: 692 us -> 0 us
  blocking collectives: 193 us -> 0 us
  Pallas kernels: 0 us -> 71.9 us
  local copies, waits for them, and re-layouts: 49.7 us -> 0 us
  other arithmetic: 32.9 us -> 0 us
  matrix products: 18.7 us -> 0 us
  between operations: 16.8 us -> 0.64 us
    reduce_scatter x1 -> x0, waiting for transfers between devices: 692 us -> none  [body(): lax.psum_scatter(terms, ('tm', 'space'), scatter_dimension=0, tiled=True)[0]]
    all_gather x8 -> x0, blocking collectives: 193 us -> none  [entering(): pieces = jax.tree.map(lambda part: lax.all_gather(part, axis), value)]
    pallas_call x0 -> x2, Pallas kernels: none -> 71.9 us  [the longest x1 69.6 us: body(): pl.pallas_call(kernel, out_shape=[block] * 7 + [jax.ShapeDtypeStruct((2,...]
    transpose x1 -> x0, local copies, waits for them, and re-layouts: 33.4 us -> none  [body(): jnp.einsum('tsc,cnk->tnsk', own_slab, own_basis, preferred_element_type=j...]
    select_n x62 -> x0, other arithmetic: 21.8 us -> none  [turn(): jnp.where(position < mine, new, old)]
    dot_general x1 -> x0, matrix products: 18.7 us -> none  [body(): jnp.einsum('tsc,cnk->tnsk', own_slab, own_basis, preferred_element_type=j...]
    slice x220 -> x0, local copies, waits for them, and re-layouts: 10.3 us -> none  [the longest x131 6.92 us: body(): local_prefix = lax.associative_scan(filter_combine, elements, axis=0)]
  transfers between devices with their start and end apart: 2 -> 0, of which waited for: 1 -> 0; matrix products, arithmetic and copies ran while one was open for 4% -> 0% of each run, Pallas kernels for 0% -> 0%
where the time goes in v2:
time: 72.7 us; the launch traced here: 72.5 us
  Pallas kernels  71.9 us (99%)
    pallas_call x1, Pallas kernels, body(): pl.pallas_call(kernel, out_shape=[block] * 7 + [jax.ShapeDtypeStruct((2,...  69.6 us
    pallas_call x1, Pallas kernels, body(): pl.pallas_call(apply_starts, out_shape=[block] * 4, in_specs=[anywhere] *...  2.29 us

profile of v2, /device:TPU:1, one launch (start us, length us, event | category | flops | bytes accessed | tf_op | source)
XLA Modules:
  0.0 72.5 jit_solution(12073240274184528472)
XLA Ops:
  0.6 69.6 %shard_map.111 = (f32[256,256]{1,0:T(8,128)}, f32[256,256]{1,0:T(8,128)}, f32[256,256]{1,0:T(8,128)}, f32[256,256]{1,0:T(8,128)}, f32[256,256]{1,0:T(8,128)}, /*...) custom-call(bf16[4,4,2,256,512]{4,3,2,1,0:T(8,128)(2,1)} %bitcast.8, bf16[32,512,1024]{2,1,0:T(8,128)(2,1)} %bitcast.7, ...), custom_call_target="tpu_custom_call" | custom-call | tf_op jit(solution)/shard_map/pallas_call | solution.py:663
  70.2 2.3 %shard_map.112 = (f32[256,256]{1,0:T(8,128)}, f32[256,256]{1,0:T(8,128)}, f32[256,256]{1,0:T(8,128)}, f32[256,256]{1,0:T(8,128)}) custom-call(f32[256,256]{1,0:T(8,128)} %get-tuple-element.12.refs_0_, f32[256,256]{1,0:T(8,128)} %get-tuple-element.13.refs_1_, f32[256,256]{1,0:T(8,128)} %get-tuple-element.14.refs_2_, f32[256,256]{1,0:T(8,128)} %get-tuple-element.15.refs_3_, ...), custom_call_target="tpu_custom_call" | custom-call | tf_op jit(solution)/shard_map/pallas_call | solution.py:683

commit v3 on v2

--- a/solution.py
+++ b/solution.py
@@ -1,3 +1,5 @@
+import functools
+
 import jax
 import jax.numpy as jnp
 from jax import lax
@@ -36,7 +38,7 @@
 def kernel(obs, basis, decay, mask, q_ref, r_ref, pm_ref, pv_ref, *refs):
     outs, scratch = refs[:8], refs[8:]
     (made, last, made_sem, fa, fb, fc, qa, qb, qc, ra1, ra2, ra3, rb1, rb2, rb3, rc1, rc2, rc3, oa, ob, oc, bas, scale_out, scale_in,
-     dec, flag, qv, vv, aa, kk, gg, ww, ap, sm, gs, sv, cc, ll, s0, small, e1, e2, e3, g1, g2, g3, wm, ws, wl,
+     dec, flag, qv, vv, aa, kk, gg, ww, ap, sm, gs, sv, cc, ll, s0, al, be, small, e1, e2, e3, g1, g2, g3, wm, ws, wl,
      own_sem, part_sem, psend_sem, bas_sem, send_sem, recv_sem, ssend_sem, srecv_sem, esend_sem, erecv_sem) = scratch
     def put(i):
         source = last if i == 7 else made.at[i]
@@ -145,16 +147,19 @@
 
     pl.semaphore_wait(barrier, 33)
 
-    for part, slot in tasks:
-        for (xi, zi), rows, to in obs_copies(part, slot):
-            pltpu.make_async_remote_copy(
-                obs.at[xi, zi, 1 - core, rows],
-                to.at[:, 512:1024],
-                psend_sem.at[part, slot],
-                part_sem.at[part, slot],
-                device_id={"tm": partner},
-                device_id_type=MESH,
-            ).start()
+    def exchange(*pieces):
+        for part, slot in pieces:
+            for (xi, zi), rows, to in obs_copies(part, slot):
+                pltpu.make_async_remote_copy(
+                    obs.at[xi, zi, 1 - core, rows],
+                    to.at[:, 512:1024],
+                    psend_sem.at[part, slot],
+                    part_sem.at[part, slot],
+                    device_id={"tm": partner},
+                    device_id_type=MESH,
+                ).start()
+
+    exchange(*tasks)
 
     def scatter(number, mine, gathered):
         gathered[tm] = mine[...]
@@ -185,7 +190,7 @@
 
     def product(part, slot, j):
         u = UNIT[part]
-        obs_slot, mode_slot = (j, slot) if part == 1 else (slot, j)
+        obs_slot, mode_slot = (j, slot) if part == 1 else (slot, j if part == 0 else lax.rem(4 - j, 4))
         return jnp.dot(held[part][obs_slot].reshape(4 * u, 1024), bas[mode_slot], preferred_element_type=F32)
 
     def place(part, stage, message, j):
@@ -212,7 +217,7 @@
 
     def copies(part, stage, message, j):
         begin, rows = place(part, stage, message, j)
-        to = neighbour(ORDER[part][stage], MESSAGES[message][2])
+        to = neighbour(ORDER[part][stage], -MESSAGES[message][2] if (part, stage) == (2, 1) else MESSAGES[message][2])
         number = number_of(part, stage, message, j)
         return (
             pltpu.make_async_remote_copy(
@@ -442,6 +447,45 @@
         for i in (2, 4, 5, 6):
             put(i).start()
 
+    def functionals():
+        def gains_before(s, carry):
+            out = []
+            for (g, h), gamma in zip(blocks, carry):
+                s0[h, steps(s, g), :] = gamma * ww[h, steps(s, g), :]
+                out.append(gamma * gg[h, steps(s, g), :])
+            return tuple(out)
+
+        lax.fori_loop(0, 16, gains_before, (one,) * 4, unroll=2)
+
+        def effects(i, carry):
+            s = 15 - i
+            out = []
+            for (g, h), (after, effect) in zip(blocks, carry):
+                a = aa[h, steps(s, g), :]
+                effect = s0[h, steps(s, g), :] + effect
+                al[h, steps(s, g), :] = after
+                be[h, steps(s, g), :] = effect
+                out.append((after * a, effect * a))
+            return tuple(out)
+
+        lax.fori_loop(0, 16, effects, ((one, nil),) * 4, unroll=2)
+        for h in range(2):
+            gamma, gammas = unit, []
+            for k in range(16):
+                gammas.append(gamma)
+                gamma = gamma * small[6, h, k : k + 1, :]
+            onward, pull = unit, zero
+            for k in range(15, -1, -1):
+                rows, at = slice(k * 16, k * 16 + 16), slice(k, k + 1)
+                after = al[h, rows, :]
+                left, right = after * onward, gammas[k] * be[h, rows, :] + after * pull
+                if k == 0:
+                    small[14, h, 0:1, :], small[15, h, 0:1, :] = left[0:1], right[0:1]
+                al[h, rows, :] = left * kk[h, rows, :]
+                be[h, rows, :] = right * kk[h, rows, :]
+                pull = gammas[k] * small[5, h, at, :] + small[4, h, at, :] * pull
+                onward = onward * small[4, h, at, :]
+
     for yr in range(4):
         pltpu.make_async_copy(bas.at[yr], bas.at[yr], bas_sem.at[yr]).wait()
 
@@ -473,7 +517,6 @@
 
         pl.when(i == 0)(variances)
         pl.when(i == 1)(smoother)
-        pl.when(i == 2)(weights)
 
         @pl.when((i >= 1) & (i < 4))
         def _():
@@ -499,6 +542,8 @@
         return carry
 
     lax.fori_loop(0, 4, round_of, 0)
+    weights()
+    functionals()
 
     for part in TURNS:
         finish(part, (0, 1))
@@ -507,19 +552,27 @@
     for part in TURNS:
         send(part, 2, 2, relayed=0)
         send(part, 2, 5, relayed=1)
+    ends, heads = [nil, nil], [nil, nil]
     for part in TURNS:
         finish(part, (2,))
         rows = slice(START[part], START[part] + UNIT[part])
         block = acc[part][0 : UNIT[part], :]
         made[0, rows, :] = block
         for h in range(2):
-            cc[h, rows, :] = block[:, lane(h)] * kk[h, rows, :]
-    put(0).start()
+            half = block[:, lane(h)]
+            cc[h, rows, :] = half * kk[h, rows, :]
+            ends[h] = ends[h] + jnp.sum((half * al[h, rows, :]).reshape(-1, 8, 128), axis=0)
+            heads[h] = heads[h] + jnp.sum((half * be[h, rows, :]).reshape(-1, 8, 128), axis=0)
 
     for h in range(2):
         pv, r = pv_ref[:, lane(h)], r_ref[:, lane(h)]
         retain = (r + (1.0 - flag[0:1, :]) * pv) / (pv + r)
-        cc[h, 0:1, :] = cc[h, 0:1, :] + jnp.where(first, retain * pm_ref[:, lane(h)], 0.0)
+        prior = jnp.where(first, retain * pm_ref[:, lane(h)], 0.0)
+        cc[h, 0:1, :] = cc[h, 0:1, :] + prior
+        e3[0:1, lane(h)] = jnp.sum(ends[h], axis=0, keepdims=True) + small[14, h, 0:1, :] * prior
+        e3[1:2, lane(h)] = jnp.sum(heads[h], axis=0, keepdims=True) + small[15, h, 0:1, :] * prior
+    scatter(2, e3, g3)
+    put(0).start()
 
     def mean_forward(s, carry):
         out = []
@@ -551,8 +604,6 @@
             back[h][k] = s
             front = fronts[k // 8 * 2 + h][k % 8 : k % 8 + 1]
             s = front + small[5, h, k : k + 1, :] * into[h][k] + small[6, h, k : k + 1, :] * s
-        e3[0:1, lane(h)], e3[1:2, lane(h)] = m, s
-    scatter(2, e3, g3)
     for h in range(2):
         for k in range(16):
             rows = slice(k * 16, k * 16 + 16)
@@ -640,8 +691,8 @@
         pltpu.VMEM((108, 1, 256), F32),
         pltpu.VMEM((2, 288, 128), F32),
         pltpu.VMEM((256, 128), F32),
-        *[plane] * 13,
-        pltpu.VMEM((14, 2, 16, 128), F32),
+        *[plane] * 15,
+        pltpu.VMEM((16, 2, 16, 128), F32),
         pltpu.VMEM((4, 256), F32),
         pltpu.VMEM((4, 256), F32),
         pltpu.VMEM((2, 256), F32),

time: 72.7 us -> 70 us (0.963)
  Pallas kernels: 71.9 us -> 69.2 us
    pallas_call x1, Pallas kernels: 69.6 us -> 66.9 us  [body(): pl.pallas_call(kernel, out_shape=[block] * 7 + [jax.ShapeDtypeStruct((2,...]
where the time goes in v3:
time: 70 us; the launch traced here: 69.8 us
  Pallas kernels  69.2 us (99%)
    pallas_call x1, Pallas kernels, body(): pl.pallas_call(kernel, out_shape=[block] * 7 + [jax.ShapeDtypeStruct((2,...  66.9 us
    pallas_call x1, Pallas kernels, body(): pl.pallas_call(apply_starts, out_shape=[block] * 4, in_specs=[anywhere] *...  2.29 us

profile of v3, /device:TPU:1, one launch (start us, length us, event | category | flops | bytes accessed | tf_op | source)
XLA Modules:
  0.0 69.8 jit_solution(1162749623661106635)
XLA Ops:
  0.6 66.9 %shard_map.111 = (f32[256,256]{1,0:T(8,128)}, f32[256,256]{1,0:T(8,128)}, f32[256,256]{1,0:T(8,128)}, f32[256,256]{1,0:T(8,128)}, f32[256,256]{1,0:T(8,128)}, /*...) custom-call(bf16[4,4,2,256,512]{4,3,2,1,0:T(8,128)(2,1)} %bitcast.8, bf16[32,512,1024]{2,1,0:T(8,128)(2,1)} %bitcast.7, ...), custom_call_target="tpu_custom_call" | custom-call | tf_op jit(solution)/shard_map/pallas_call | solution.py:714
  67.5 2.3 %shard_map.112 = (f32[256,256]{1,0:T(8,128)}, f32[256,256]{1,0:T(8,128)}, f32[256,256]{1,0:T(8,128)}, f32[256,256]{1,0:T(8,128)}) custom-call(f32[256,256]{1,0:T(8,128)} %get-tuple-element.12.refs_0_, f32[256,256]{1,0:T(8,128)} %get-tuple-element.13.refs_1_, f32[256,256]{1,0:T(8,128)} %get-tuple-element.14.refs_2_, f32[256,256]{1,0:T(8,128)} %get-tuple-element.15.refs_3_, ...), custom_call_target="tpu_custom_call" | custom-call | tf_op jit(solution)/shard_map/pallas_call | solution.py:734

commit v4 on v3

--- a/solution.py
+++ b/solution.py
@@ -19,6 +19,8 @@
 LIMIT = 32760.0
 TINY = 1e-33
 TURNS = (0, 2, 1)
+
+LAST = (2, 1, 3)
 
 MESSAGES = ((2, 0, 1), (2, 1, -1), (1, 0, 1), (1, 1, 1), (3, 0, -1), (3, 1, -1))
 
@@ -196,11 +198,11 @@
     def place(part, stage, message, j):
         slot, half, _ = MESSAGES[message]
         u = UNIT[part]
+        if stage == 2:
+            return LAST[message] * u, u
         if stage == 0:
             return (slot * 4 + j) * (4 * u) + half * (2 * u), 2 * u
-        if stage == 1:
-            return slot * 4 * u + half * 2 * u, 2 * u
-        return slot * u + half * (u // 2), u // 2
+        return slot * 4 * u + half * 2 * u, 2 * u
 
     def number_of(part, stage, message, j):
         return part * 36 + (j * 6 if stage == 0 else 18 + 6 * stage) + message
@@ -217,7 +219,12 @@
 
     def copies(part, stage, message, j):
         begin, rows = place(part, stage, message, j)
-        to = neighbour(ORDER[part][stage], -MESSAGES[message][2] if (part, stage) == (2, 1) else MESSAGES[message][2])
+        if stage == 2:
+            slot = LAST[message]
+            to = {"tm": turn(tm, 8 * slot, 32) if ORDER[part][2] == "x" else x * 8 + turn(z, slot, 4) * 2 + core}
+        else:
+            way = MESSAGES[message][2]
+            to = neighbour(ORDER[part][stage], -way if (part, stage) == (2, 1) else way)
         number = number_of(part, stage, message, j)
         return (
             pltpu.make_async_remote_copy(
@@ -245,7 +252,7 @@
     def send(part, stage, message, j=0, relayed=None):
         begin, rows = place(part, stage, message, j)
         number = number_of(part, stage, message, j)
-        size = min(rows, 64)
+        size = rows if stage == 2 else 64
         if relayed is not None:
             recv_wait(part, stage, relayed, j)
             factor = scale_in[number_of(part, stage, relayed, j)]
@@ -297,9 +304,8 @@
 
     def finish(part, stages, j=0):
         u = UNIT[part]
-        rows = u // 2 if stages == (2,) else 2 * u
-        size = min(rows, 64)
-        for half, pair in enumerate(((2, 4), (3, 5))):
+        rows, size = (u, u) if stages == (2,) else (2 * u, 64)
+        for half, pair in enumerate(((0, 1, 2),) if stages == (2,) else ((2, 4), (3, 5))):
             begin = half * rows + (j * (4 * u) if stages == (0,) else 0)
             came = [(stage, message) for stage in stages for message in pair]
             for stage, message in came:
@@ -547,11 +553,8 @@
 
     for part in TURNS:
         finish(part, (0, 1))
-        for message in (0, 1, 3, 4):
+        for message in range(3):
             send(part, 2, message)
-    for part in TURNS:
-        send(part, 2, 2, relayed=0)
-        send(part, 2, 5, relayed=1)
     ends, heads = [nil, nil], [nil, nil]
     for part in TURNS:
         finish(part, (2,))
@@ -614,7 +617,7 @@
     for part in range(3):
         u = UNIT[part]
         for stage, (begin, rows, base, count) in enumerate(
-            ((16 * u, 48 * u, 0, 24), (4 * u, 12 * u, 24, 6), (u, 3 * u, 30, 6))
+            ((16 * u, 48 * u, 0, 24), (4 * u, 12 * u, 24, 6), (u, 3 * u, 30, 3))
         ):
             some = quant[part].at[pl.ds(begin, rows)]
             pltpu.make_async_copy(some, some, send_sem.at[part, stage]).wait()
@@ -675,7 +678,7 @@
     anywhere = pl.BlockSpec(memory_space=pl.ANY)
     plane = pltpu.VMEM((2, 256, 128), F32)
     landing = [
-        pltpu.VMEM(shape, I16) for u in UNIT for shape in ((24, 2 * u, 256), (6, 2 * u, 256), (6, u // 2, 256))
+        pltpu.VMEM(shape, I16) for u in UNIT for shape in ((24, 2 * u, 256), (6, 2 * u, 256), (3, u, 256))
     ]
     dma = pltpu.SemaphoreType.DMA
     scratch = [

time: 70 us -> 68.6 us (0.980)
  Pallas kernels: 69.2 us -> 67.8 us
    pallas_call x1, Pallas kernels: 66.9 us -> 65.5 us  [body(): pl.pallas_call(kernel, out_shape=[block] * 7 + [jax.ShapeDtypeStruct((2,...]
where the time goes in v4:
time: 68.6 us; the launch traced here: 68.4 us
  Pallas kernels  67.8 us (99%)
    pallas_call x1, Pallas kernels, body(): pl.pallas_call(kernel, out_shape=[block] * 7 + [jax.ShapeDtypeStruct((2,...  65.5 us
    pallas_call x1, Pallas kernels, body(): pl.pallas_call(apply_starts, out_shape=[block] * 4, in_specs=[anywhere] *...  2.29 us

profile of v4, /device:TPU:1, one launch (start us, length us, event | category | flops | bytes accessed | tf_op | source)
XLA Modules:
  0.0 68.4 jit_solution(5522940286325874150)
XLA Ops:
  0.6 65.5 %shard_map.111 = (f32[256,256]{1,0:T(8,128)}, f32[256,256]{1,0:T(8,128)}, f32[256,256]{1,0:T(8,128)}, f32[256,256]{1,0:T(8,128)}, f32[256,256]{1,0:T(8,128)}, /*...) custom-call(bf16[4,4,2,256,512]{4,3,2,1,0:T(8,128)(2,1)} %bitcast.8, bf16[32,512,1024]{2,1,0:T(8,128)(2,1)} %bitcast.7, ...), custom_call_target="tpu_custom_call" | custom-call | tf_op jit(solution)/shard_map/pallas_call | solution.py:717
  66.1 2.3 %shard_map.112 = (f32[256,256]{1,0:T(8,128)}, f32[256,256]{1,0:T(8,128)}, f32[256,256]{1,0:T(8,128)}, f32[256,256]{1,0:T(8,128)}) custom-call(f32[256,256]{1,0:T(8,128)} %get-tuple-element.12.refs_0_, f32[256,256]{1,0:T(8,128)} %get-tuple-element.13.refs_1_, f32[256,256]{1,0:T(8,128)} %get-tuple-element.14.refs_2_, f32[256,256]{1,0:T(8,128)} %get-tuple-element.15.refs_3_, ...), custom_call_target="tpu_custom_call" | custom-call | tf_op jit(solution)/shard_map/pallas_call | solution.py:737
